TPU v7x, 256 devices: a whole 4x4x8 slice. The times are simulated.
256 devices in a mesh: out: 128 (over z, y, x), con: 2 (over core).
Axes of the slice: x: 4, y: 4, z: 8, core: 2. Of those that a mesh axis runs over, the one named last changes fastest.
Arguments:
- amplitudes: bfloat16 [512, 9216], P(('out', 'con')), may hold values from -6 to 6
- integrals: bfloat16 [131072, 9216], P('out', 'con'), may hold values from -0.078125 to 0.078125
- block_sizes: int32 [8], replicated, may hold values from 64 to 192, as said below
Outputs:
- ladder: bfloat16 [512, 131072], P('con', 'out')
Inputs may be any that keep to these rules, and one draw needn't show every extreme that they name: `block_sizes`: each entry lies between 64 and 192; the entries sum to 1024; one entry equals 192 and one equals 64.
All inputs are finite; a program needn't handle non-finite values.
Results may differ from a plain program's by a relative error of at most 0.001.
Values may be sent and summed in bfloat16 or wider, within the bound.
A program may use at most 64 MiB of HBM per device.

v0:
```python
import jax
import jax.numpy as jnp
from jax import lax
from jax.sharding import PartitionSpec as P

DMAX = 192


def mask_slots(amplitudes, block_sizes):
    row_count = amplitudes.shape[0]
    nirrep = block_sizes.shape[0]
    blocked = amplitudes.reshape(row_count, nirrep, -1, DMAX)
    valid_cols = jnp.arange(DMAX, dtype=jnp.int32)[None, :] < block_sizes[:, None]
    masked = jnp.where(valid_cols[None, :, None, :], blocked, jnp.zeros((), amplitudes.dtype))
    return masked.reshape(row_count, -1)


def contract(amp_rows, integrals):
    return lax.dot_general(
        amp_rows, integrals, (((1,), (1,)), ((), ())), preferred_element_type=jnp.float32
    )


def on_device(amplitudes, integrals, block_sizes):
    masked = mask_slots(amplitudes, block_sizes)
    gathered = lax.all_gather(masked, "out", axis=0, tiled=True)
    own_columns = lax.all_to_all(gathered, "con", split_axis=1, concat_axis=0, tiled=True)
    out_count = lax.axis_size("out")
    con_count = lax.axis_size("con")
    per_device = masked.shape[0]
    own_columns = own_columns.reshape(con_count, out_count, per_device, -1)
    own_columns = jnp.transpose(own_columns, (1, 0, 2, 3)).reshape(
        con_count * out_count * per_device, -1
    )
    partial_sums = contract(own_columns, integrals)
    ladder = lax.psum_scatter(partial_sums, "con", scatter_dimension=0, tiled=True)
    return ladder.astype(jnp.bfloat16)


def solution(mesh):
    in_specs = (P(("out", "con"), None), P("out", "con"), P())
    out_specs = P("con", "out")
    return jax.shard_map(
        on_device, mesh=mesh, in_specs=in_specs, out_specs=out_specs, check_vma=False
    )
```

profile of v0, /device:TPU:1, one launch (start us, length us, event | category | flops | bytes accessed | tf_op | source)
XLA Modules:
  0.0 213.8 jit_solution(9035128441927319287)
XLA Ops:
  6.5 0.0 all-gather.3.cloned.1.call-start
  6.5 0.7 iota_compare_fusion
  7.3 0.1 broadcast_in_dim.20
  7.4 1.5 fusion
  8.8 0.0 all-gather.3.cloned.1.call-update
  8.9 0.0 reduce-scatter.2.cloned.1.call-start
  8.9 120.1 %all-gather.3.cloned.1.call-done = bf16[128,2,9216]{2,1,0:T(2,128)(2,1)} async-done(((bf16[1,2,9216]{2,1,0:T(2,128)(2,1)}), bf16[128,2,9216]{2,1,0:T(2,128)(2,1)}) %all-gather.3.cloned.1.call-update) | async-done | bytes 4718608 | tf_op jit(solution)/shard_map/all_gather | solution.py:26
  129.0 13.5 %all_to_all.12 = bf16[256,2,4608]{2,1,0:T(2,128)(2,1)} reshape(bf16[128,2,9216]{2,1,0:T(2,128)(2,1)} %all-gather.3.cloned.1.call-done) | data formatting | bytes 9437184 | tf_op jit(solution)/shard_map/all_to_all | solution.py:27
  142.5 2.8 %copy.5 = bf16[256,2,4608]{2,0,1:T(8,128)(2,1)S(1)} copy(bf16[256,2,4608]{2,1,0:T(2,128)(2,1)} %all_to_all.12) | data formatting | bytes 9437184 | tf_op jit(solution)/shard_map/all_to_all | solution.py:27
  145.3 12.7 %all_to_all.16 = bf16[256,2,4608]{2,0,1:T(8,128)(2,1)} all-to-all(bf16[256,2,4608]{2,0,1:T(8,128)(2,1)S(1)} %copy.5), channel_id=1, replica_groups=mesh['out'=128,'con'=2] {'con'}, dimensions={1} | all-to-all | bytes 9437184 | tf_op jit(solution)/shard_map/all_to_all | solution.py:27
  158.1 9.3 %copy.6 = bf16[2,256,4608]{2,0,1:T(2,128)(2,1)} copy(bf16[2,256,4608]{2,1,0:T(8,128)(2,1)} %bitcast.8) | data formatting | bytes 9437184 | tf_op jit(solution)/shard_map/all_to_all | solution.py:27
  167.4 8.2 %copy.7 = bf16[128,2,2,4608]{3,2,1,0:T(2,128)(2,1)} copy(bf16[128,2,2,4608]{3,1,2,0:T(2,128)(2,1)} %bitcast.9) | data formatting | bytes 9437184 | tf_op jit(solution)/shard_map/transpose | solution.py:32
  175.6 7.6 %reshape.32 = bf16[512,4608]{1,0:T(8,128)(2,1)} reshape(bf16[128,2,2,4608]{3,2,1,0:T(2,128)(2,1)} %copy.7) | data formatting | bytes 9437184 | tf_op jit(solution)/shard_map/reshape | solution.py:32
  183.2 10.1 %fusion.1 = f32[512,1024]{1,0:T(8,128)} fusion(bf16[512,4608]{1,0:T(8,128)(2,1)} %reshape.32, bf16[1024,4608]{1,0:T(8,128)(2,1)} %param.4), kind=kOutput, calls=%fused_computation.3 | convolution fusion | flops 4831838208 | bytes 16252928 | tf_op jit(solution)/shard_map/dot_general | solution.py:19
  193.2 0.0 reduce-scatter.2.cloned.1.call-update
  193.2 11.6 %reduce-scatter.2.cloned.1.call-done = f32[256,1024]{1,0:T(8,128)} async-done(((f32[512,1024]{1,0:T(8,128)}), f32[256,1024]{1,0:T(8,128)}) %reduce-scatter.2.cloned.1.call-update) | async-done | bytes 1048592 | tf_op jit(solution)/shard_map/reduce_scatter | solution.py:36
  204.9 2.1 convert_element_type.3
  (1 shorter events, 0.0 us)
Async XLA Ops:
  6.5 122.5 %all-gather.3.cloned.1.call-start = ((), (), s32[]{:S(2)}) async-start(), calls=%async_computation.3 | async-start | bytes 4755456 | tf_op jit(solution)/shard_map/all_gather | solution.py:26
  8.9 196.0 %reduce-scatter.2.cloned.1.call-start = ((), (), s32[]{:S(2)}) async-start(), calls=%async_computation.2 | async-start | bytes 3145728 | tf_op jit(solution)/shard_map/reduce_scatter | solution.py:36
Sparse Core Ops, SparseCore 0:
  11.2 117.7 all-gather.2
  193.4 11.4 reduce-scatter.1
where the time goes:
time: 215 us; the launch traced here: 214 us
  waiting for transfers between devices  132 us (61%)
  local copies, waits for them, and re-layouts  41.5 us (19%)
  between operations  13.4 us (6%)
  blocking collectives  12.7 us (6%)
  matrix products  10.1 us (5%)
  other arithmetic  4.27 us (2%)
    all_gather x1, waiting for transfers between devices, on_device(): gathered = lax.all_gather(masked, 'out', axis=0, tiled=True)  120 us
    all_to_all x3, local copies, waits for them, and re-layouts, on_device(): lax.all_to_all(gathered, 'con', split_axis=1, concat_axis=0, tiled=True)  25.6 us
    all_to_all x1, blocking collectives, on_device(): lax.all_to_all(gathered, 'con', split_axis=1, concat_axis=0, tiled=True)  12.7 us
    reduce_scatter x1, waiting for transfers between devices, on_device(): lax.psum_scatter(partial_sums, 'con', scatter_dimension=0, tiled=True)  11.6 us
    dot_general x1, matrix products, contract(): lax.dot_general(amp_rows, integrals, (((1,), (1,)), ((), ())), preferred_...  10.1 us
    transpose x1, local copies, waits for them, and re-layouts, on_device(): jnp.transpose(own_columns, (1, 0, 2, 3))  8.22 us
    reshape x1, local copies, waits for them, and re-layouts, on_device(): jnp.transpose(own_columns, (1, 0, 2, 3))  7.55 us
  transfers between devices with their start and end apart: 2, of which 2 were waited for; matrix products, arithmetic and copies ran while one was open for 0% of the time, Pallas kernels for 0%

commit v1 on v0

--- a/solution.py
+++ b/solution.py
@@ -23,18 +23,23 @@
 
 def on_device(amplitudes, integrals, block_sizes):
     masked = mask_slots(amplitudes, block_sizes)
-    gathered = lax.all_gather(masked, "out", axis=0, tiled=True)
-    own_columns = lax.all_to_all(gathered, "con", split_axis=1, concat_axis=0, tiled=True)
-    out_count = lax.axis_size("out")
+    con = lax.axis_index("con")
     con_count = lax.axis_size("con")
-    per_device = masked.shape[0]
-    own_columns = own_columns.reshape(con_count, out_count, per_device, -1)
-    own_columns = jnp.transpose(own_columns, (1, 0, 2, 3)).reshape(
-        con_count * out_count * per_device, -1
+    half = integrals.shape[1]
+    chip_rows = lax.all_gather(masked, "con", axis=0, tiled=True)
+    own_cols = lax.dynamic_slice_in_dim(chip_rows, con * half, half, axis=1)
+    all_rows = lax.all_gather(own_cols, "out", axis=0, tiled=True)
+    out_rows = all_rows.shape[0] // con_count
+    other = 1 - con
+    other_part = contract(
+        lax.dynamic_slice_in_dim(all_rows, other * out_rows, out_rows, axis=0), integrals
     )
-    partial_sums = contract(own_columns, integrals)
-    ladder = lax.psum_scatter(partial_sums, "con", scatter_dimension=0, tiled=True)
-    return ladder.astype(jnp.bfloat16)
+    received = lax.ppermute(other_part, "con", perm=[(0, 1), (1, 0)])
+    own_part = contract(
+        lax.dynamic_slice_in_dim(all_rows, con * out_rows, out_rows, axis=0), integrals
+    )
+    own_part = lax.optimization_barrier(own_part)
+    return (own_part + received).astype(jnp.bfloat16)
 
 
 def solution(mesh):

time: 215 us -> 161 us (0.75)
  local copies, waits for them, and re-layouts: 41.5 us -> 8.04 us
  waiting for transfers between devices: 132 us -> 115 us
  blocking collectives: 12.7 us -> 4.75 us
  starting transfers between devices: 0.04 us -> 4.49 us
    all_to_all x3 -> x0, local copies, waits for them, and re-layouts: 25.6 us -> none  [on_device(): lax.all_to_all(gathered, 'con', split_axis=1, concat_axis=0, tiled=True)]
    all_to_all x1 -> x0, blocking collectives: 12.7 us -> none  [on_device(): lax.all_to_all(gathered, 'con', split_axis=1, concat_axis=0, tiled=True)]
    reduce_scatter x1 -> x0, waiting for transfers between devices: 11.6 us -> none  [on_device(): lax.psum_scatter(partial_sums, 'con', scatter_dimension=0, tiled=True)]
    transpose x1 -> x0, local copies, waits for them, and re-layouts: 8.22 us -> none  [on_device(): jnp.transpose(own_columns, (1, 0, 2, 3))]
    unnamed x0 -> x3, local copies, waits for them, and re-layouts: none -> 7.92 us
    reshape x1 -> x0, local copies, waits for them, and re-layouts: 7.55 us -> none  [on_device(): jnp.transpose(own_columns, (1, 0, 2, 3))]
    all_gather x1, waiting for transfers between devices: 120 us -> 115 us  [on_device(): all_rows = lax.all_gather(own_cols, 'out', axis=0, tiled=True)]
    all_gather x0 -> x1, blocking collectives: none -> 4.75 us  [on_device(): chip_rows = lax.all_gather(masked, 'con', axis=0, tiled=True)]
  transfers between devices with their start and end apart: 2 -> 2, of which waited for: 2 -> 1; matrix products, arithmetic and copies ran while one was open for 0% -> 4% of each run, Pallas kernels for 0% -> 0%
where the time goes in v1:
time: 161 us; the launch traced here: 160 us
  waiting for transfers between devices  115 us (71%)
  between operations  13.4 us (8%)
  matrix products  11.9 us (7%)
  local copies, waits for them, and re-layouts  8.04 us (5%)
  blocking collectives  4.75 us (3%)
  starting transfers between devices  4.49 us (3%)
  other arithmetic  2.51 us (2%)
    all_gather x1, waiting for transfers between devices, on_device(): all_rows = lax.all_gather(own_cols, 'out', axis=0, tiled=True)  115 us
    dot_general x2, matrix products, contract(): lax.dot_general(amp_rows, integrals, (((1,), (1,)), ((), ())), preferred_...  11.9 us
    unnamed x3, local copies, waits for them, and re-layouts  7.92 us
    all_gather x1, blocking collectives, on_device(): chip_rows = lax.all_gather(masked, 'con', axis=0, tiled=True)  4.75 us
    ppermute x1, starting transfers between devices, on_device(): received = lax.ppermute(other_part, 'con', perm=[(0, 1), (1, 0)])  4.49 us
  transfers between devices with their start and end apart: 2, of which 1 were waited for; matrix products, arithmetic and copies ran while one was open for 4% of the time, Pallas kernels for 0%

profile of v1, /device:TPU:1, one launch (start us, length us, event | category | flops | bytes accessed | tf_op | source)
XLA Modules:
  0.0 160.5 jit_solution(4676826917405376229)
XLA Ops:
  6.5 0.0 all-gather.4.cloned.1.call-start
  6.5 0.7 iota_compare_fusion
  7.3 0.1 broadcast_in_dim.20
  7.4 0.8 fusion.4
  8.2 4.8 %all-gather = bf16[2,2,9216]{2,1,0:T(2,128)(2,1)S(1)} all-gather(bf16[1,2,9216]{2,1,0:T(2,128)(2,1)S(1)} %fusion.4), channel_id=1, replica_groups=mesh['out'=128,'con'=2] {'con'}, dimensions={0}, use_global_device_ids=true | all-gather | bytes 110592 | tf_op jit(solution)/shard_map/all_gather | solution.py:29
  13.0 0.6 dynamic-slice_bitcast_fusion
  13.7 0.0 all-gather.4.cloned.1.call-update
  13.7 115.3 %all-gather.4.cloned.1.call-done = bf16[128,4,4608]{2,1,0:T(4,128)(2,1)} async-done(((bf16[1,4,4608]{2,1,0:T(4,128)(2,1)}), bf16[128,4,4608]{2,1,0:T(4,128)(2,1)}) %all-gather.4.cloned.1.call-update) | async-done | bytes 4718608 | tf_op jit(solution)/shard_map/all_gather | solution.py:31
  129.0 7.2 %reshape.24 = bf16[512,4608]{1,0:T(8,128)(2,1)} reshape(bf16[128,4,4608]{2,1,0:T(4,128)(2,1)} %all-gather.4.cloned.1.call-done) | data formatting | bytes 9437184
  136.2 6.0 %fusion = f32[256,1024]{1,0:T(8,128)S(1)} fusion(bf16[1024,4608]{1,0:T(8,128)(2,1)} %param.4, bf16[512,4608]{1,0:T(8,128)(2,1)} %reshape.24, s32[]{:T(128)S(6)} %select_n.17), kind=kOutput, calls=%fused_computation | convolution fusion | flops 2415919104 | bytes 12845060 | tf_op jit(solution)/shard_map/dot_general | solution.py:19
  142.2 4.5 %collective-permute-start = (f32[256,1024]{1,0:T(8,128)S(1)}, f32[256,1024]{1,0:T(8,128)S(1)}, u32[]{:S(2)}, u32[]{:S(2)}) collective-permute-start(f32[256,1024]{1,0:T(8,128)S(1)} %fusion), channel_id=1, source_target_pairs={{0,1},{1,0},{2,3},{3,2},{4,5},{5,4},{6,7},{7,6},{8,9},{9,8},{10,11... | collective-permute-start | bytes 3145736 | tf_op jit(solution)/shard_map/ppermute | solution.py:37
  146.7 6.0 %fusion.2 = f32[256,1024]{1,0:T(8,128)S(1)} fusion(bf16[1024,4608]{1,0:T(8,128)(2,1)} %param.4, bf16[512,4608]{1,0:T(8,128)(2,1)} %reshape.24, s32[]{:T(128)S(6)} %select_n.16), kind=kOutput, calls=%fused_computation.2 | convolution fusion | flops 2415919104 | bytes 12845060 | tf_op jit(solution)/shard_map/dot_general | solution.py:19
  152.7 0.0 collective-permute-done
  152.7 1.0 add_convert_fusion
  (2 shorter events, 0.0 us)
Async XLA Ops:
  6.5 122.5 %all-gather.4.cloned.1.call-start = ((), (), s32[]{:S(2)}) async-start(), calls=%async_computation | async-start | bytes 4755456 | tf_op jit(solution)/shard_map/all_gather | solution.py:31
  142.2 10.5 %collective-permute-start = (f32[256,1024]{1,0:T(8,128)S(1)}, f32[256,1024]{1,0:T(8,128)S(1)}, u32[]{:S(2)}, u32[]{:S(2)}) collective-permute-start(f32[256,1024]{1,0:T(8,128)S(1)} %fusion), channel_id=1, source_target_pairs={{0,1},{1,0},{2,3},{3,2},{4,5},{5,4},{6,7},{7,6},{8,9},{9,8},{10,11... | collective-permute-start | bytes 3145736 | tf_op jit(solution)/shard_map/ppermute | solution.py:37
Sparse Core Ops, SparseCore 0:
  13.8 115.1 all-gather.3

commit v2 on v0

v2 whole, which is shorter than its diff:
```python
import jax
import jax.numpy as jnp
from jax import lax
from jax.sharding import Mesh, PartitionSpec as P

DMAX = 192
TORUS = {128: (("z", 8), ("y", 4), ("x", 4))}


def mask_slots(amplitudes, block_sizes):
    row_count = amplitudes.shape[0]
    nirrep = block_sizes.shape[0]
    blocked = amplitudes.reshape(row_count, nirrep, -1, DMAX)
    valid_cols = jnp.arange(DMAX, dtype=jnp.int32)[None, :] < block_sizes[:, None]
    masked = jnp.where(valid_cols[None, :, None, :], blocked, jnp.zeros((), amplitudes.dtype))
    return masked.reshape(row_count, -1)


def contract(amp_rows, integrals):
    return lax.dot_general(
        amp_rows, integrals, (((1,), (1,)), ((), ())), preferred_element_type=jnp.float32
    )


def make_on_device(out_axes):
    def on_device(amplitudes, integrals, block_sizes):
        masked = mask_slots(amplitudes, block_sizes)
        con = lax.axis_index("con")
        con_count = lax.axis_size("con")
        half = integrals.shape[1]
        chip_rows = lax.all_gather(masked, "con", axis=0, tiled=True)
        all_rows = lax.dynamic_slice_in_dim(chip_rows, con * half, half, axis=1)
        for name in reversed(out_axes):
            all_rows = lax.all_gather(all_rows, name, axis=0, tiled=True)
        out_rows = all_rows.shape[0] // con_count
        other = 1 - con
        other_part = contract(
            lax.dynamic_slice_in_dim(all_rows, other * out_rows, out_rows, axis=0), integrals
        )
        received = lax.ppermute(other_part, "con", perm=[(0, 1), (1, 0)])
        own_part = contract(
            lax.dynamic_slice_in_dim(all_rows, con * out_rows, out_rows, axis=0), integrals
        )
        own_part = lax.optimization_barrier(own_part)
        return (own_part + received).astype(jnp.bfloat16)

    return on_device


def solution(mesh):
    n_out = mesh.shape["out"]
    axes = TORUS.get(n_out, (("out", n_out),))
    names = tuple(name for name, _ in axes)
    devices = mesh.devices.reshape(tuple(size for _, size in axes) + (mesh.shape["con"],))
    torus_mesh = Mesh(devices, names + ("con",))
    in_specs = (P(names + ("con",), None), P(names, "con"), P())
    out_specs = P("con", names)
    return jax.shard_map(
        make_on_device(names), mesh=torus_mesh, in_specs=in_specs, out_specs=out_specs,
        check_vma=False,
    )
```

time: 215 us -> 120 us (0.56)
  waiting for transfers between devices: 132 us -> 66.2 us
  local copies, waits for them, and re-layouts: 41.5 us -> 0.22 us
  blocking collectives: 12.7 us -> 24.7 us
    all_gather x1, waiting for transfers between devices: 120 us -> 66.2 us  [on_device(): all_rows = lax.all_gather(all_rows, name, axis=0, tiled=True)]
    all_to_all x3 -> x0, local copies, waits for them, and re-layouts: 25.6 us -> none  [on_device(): lax.all_to_all(gathered, 'con', split_axis=1, concat_axis=0, tiled=True)]
    all_gather x0 -> x3, blocking collectives: none -> 24.7 us  [the longest x2 19.9 us: on_device(): all_rows = lax.all_gather(all_rows, name, axis=0, tiled=True)]
    all_to_all x1 -> x0, blocking collectives: 12.7 us -> none  [on_device(): lax.all_to_all(gathered, 'con', split_axis=1, concat_axis=0, tiled=True)]
    reduce_scatter x1 -> x0, waiting for transfers between devices: 11.6 us -> none  [on_device(): lax.psum_scatter(partial_sums, 'con', scatter_dimension=0, tiled=True)]
    transpose x1 -> x0, local copies, waits for them, and re-layouts: 8.22 us -> none  [on_device(): jnp.transpose(own_columns, (1, 0, 2, 3))]
    reshape x1 -> x0, local copies, waits for them, and re-layouts: 7.55 us -> none  [on_device(): jnp.transpose(own_columns, (1, 0, 2, 3))]
    dot_general x1 -> x2, matrix products: 10.1 us -> 11.9 us  [contract(): lax.dot_general(amp_rows, integrals, (((1,), (1,)), ((), ())), preferred_...]
  transfers between devices with their start and end apart: 2 -> 2, of which waited for: 2 -> 1; matrix products, arithmetic and copies ran while one was open for 0% -> 5% of each run, Pallas kernels for 0% -> 0%
where the time goes in v2:
time: 120 us
  waiting for transfers between devices  66.2 us (55%)
  blocking collectives  24.7 us (21%)
  between operations  13.4 us (11%)
  matrix products  11.9 us (10%)
  other arithmetic  2.51 us (2%)
    all_gather x1, waiting for transfers between devices, on_device(): all_rows = lax.all_gather(all_rows, name, axis=0, tiled=True)  66.2 us
    all_gather x2, blocking collectives, on_device(): all_rows = lax.all_gather(all_rows, name, axis=0, tiled=True)  19.9 us
    dot_general x2, matrix products, contract(): lax.dot_general(amp_rows, integrals, (((1,), (1,)), ((), ())), preferred_...  11.9 us
    all_gather x1, blocking collectives, on_device(): chip_rows = lax.all_gather(masked, 'con', axis=0, tiled=True)  4.75 us
  transfers between devices with their start and end apart: 2, of which 1 were waited for; matrix products, arithmetic and copies ran while one was open for 5% of the time, Pallas kernels for 0%

profile of v2, /device:TPU:1, one launch (start us, length us, event | category | flops | bytes accessed | tf_op | source)
XLA Modules:
  0.0 119.7 jit_solution(11476787945079464817)
XLA Ops:
  6.5 0.0 all-gather.4.cloned.1.call-start
  6.5 0.7 iota_compare_fusion
  7.3 0.1 broadcast_in_dim.20
  7.4 0.8 fusion.4
  8.2 4.8 %all-gather = bf16[2,2,9216]{2,1,0:T(2,128)(2,1)S(1)} all-gather(bf16[1,2,9216]{2,1,0:T(2,128)(2,1)S(1)} %fusion.4), channel_id=1, replica_groups=mesh['z'=8,'y'=4,'x'=4,'con'=2] {'con'}, dimensions={0}, use_global_device_ids=true | all-gather | bytes 110592 | tf_op jit(solution)/shard_map/all_gather | solution.py:31
  13.0 9.1 %all-gather.1 = bf16[4,4,4608]{2,1,0:T(4,128)(2,1)S(1)} all-gather(bf16[1,4,4608]{2,1,0:T(4,128)(2,1)S(1)} %dynamic-slice_bitcast_fusion), channel_id=1, replica_groups=mesh['z'=8,'y'=4,'x'=4,'con'=2] {'x'}, dimensions={0}, use_global_device_ids=true | all-gather | bytes 184320 | tf_op jit(solution)/shard_map/all_gather | solution.py:34
  22.2 10.8 %all_gather.14 = bf16[64,4608]{1,0:T(8,128)(2,1)} all-gather(bf16[16,4608]{1,0:T(8,128)(2,1)S(1)} %reshape.24), channel_id=1, replica_groups=mesh['z'=8,'y'=4,'x'=4,'con'=2] {'y'}, dimensions={0}, use_global_device_ids=true | all-gather | bytes 737280 | tf_op jit(solution)/shard_map/all_gather | solution.py:34
  33.0 0.0 all-gather.4.cloned.1.call-update
  33.0 66.2 %all-gather.4.cloned.1.call-done = bf16[512,4608]{1,0:T(8,128)(2,1)} async-done(((bf16[64,4608]{1,0:T(8,128)(2,1)}), bf16[512,4608]{1,0:T(8,128)(2,1)}) %all-gather.4.cloned.1.call-update) | async-done | bytes 4718608 | tf_op jit(solution)/shard_map/all_gather | solution.py:34
  99.2 6.0 %fusion = f32[256,1024]{1,0:T(8,128)S(1)} fusion(bf16[1024,4608]{1,0:T(8,128)(2,1)} %param.4, bf16[512,4608]{1,0:T(8,128)(2,1)} %all-gather.4.cloned.1.call-done, s32[]{:T(128)S(6)} %select_n.17), kind=kOutput, calls=%fused_computation | convolution fusion | flops 2415919104 | bytes 12845060 | tf_op jit(solution)/shard_map/dot_general | solution.py:20
  105.2 0.8 collective-permute-start
  105.9 6.0 %fusion.2 = f32[256,1024]{1,0:T(8,128)S(1)} fusion(bf16[1024,4608]{1,0:T(8,128)(2,1)} %param.4, bf16[512,4608]{1,0:T(8,128)(2,1)} %all-gather.4.cloned.1.call-done, s32[]{:T(128)S(6)} %select_n.16), kind=kOutput, calls=%fused_computation.2 | convolution fusion | flops 2415919104 | bytes 12845060 | tf_op jit(solution)/shard_map/dot_general | solution.py:20
  111.9 0.0 collective-permute-done
  111.9 1.0 add_convert_fusion
  (4 shorter events, 0.1 us)
Async XLA Ops:
  6.5 92.7 %all-gather.4.cloned.1.call-start = ((), (), s32[]{:S(2)}) async-start(), calls=%async_computation | async-start | bytes 5308416 | tf_op jit(solution)/shard_map/all_gather | solution.py:34
  105.2 6.7 %collective-permute-start = (f32[256,1024]{1,0:T(8,128)S(1)}, f32[256,1024]{1,0:T(8,128)S(1)}, u32[]{:S(2)}, u32[]{:S(2)}) collective-permute-start(f32[256,1024]{1,0:T(8,128)S(1)} %fusion), channel_id=1, source_target_pairs={{0,1},{1,0},{2,3},{3,2},{4,5},{5,4},{6,7},{7,6},{8,9},{9,8},{10,11... | collective-permute-start | bytes 3145736 | tf_op jit(solution)/shard_map/ppermute | solution.py:40
Sparse Core Ops, SparseCore 0:
  33.1 66.0 all-gather.3
